TPU v7x, 256 devices: a whole 4x4x8 slice. The times are simulated.
256 devices in a mesh: group: 8 (over z_hi, core), tensor: 8 (over y, z_lo), seq: 4 (over x).
Axes of the slice: x: 4, y: 4, z: 8 (z_hi: 4, z_lo: 2; z = z_hi * 2 + z_lo), core: 2. Of those that a mesh axis runs over, the one named last changes fastest.
Arguments:
- patches: bfloat16 [8192, 1280], P(('group', 'tensor', 'seq')), may hold values from -6 to 6
- enc_gain: float32 [1280], replicated, may hold values from 0.1 to 1.9
- enc_qkv: bfloat16 [3, 1280, 1280], P(None, None, 'tensor')
- enc_out: bfloat16 [1280, 1280], P('tensor'), may hold values from -0.15625 to 0.15625
- cross_kv: bfloat16 [1280, 2048], P(None, 'tensor'), may hold values from -0.15625 to 0.15625
- key_gain: float32 [128], replicated, may hold values from 0.1 to 1.9
- dec_hidden: bfloat16 [4096, 8192], P(('group', 'seq')), may hold values from -6 to 6
- dec_gain: float32 [8192], replicated, may hold values from 0.1 to 1.9
- query_weight: bfloat16 [8192, 4096], P(None, 'tensor'), may hold values from -0.0625 to 0.0625
- query_gain: float32 [128], replicated, may hold values from 1.5 to 3
- image_of_row: int32 [4096], P(('group', 'seq')), may hold values from 0 to 3
- valid_count: int32 [4096], P(('group', 'seq')), may hold values from 1 to 2048, as said below
Outputs:
- decoded: bfloat16 [4096, 4096], P(('group', 'seq'), 'tensor')
Inputs may be any that keep to these rules, and one draw needn't show every extreme that they name: `valid_count`: every draw has a row reading a whole image and a row reading one patch.
All inputs are finite; a program needn't handle non-finite values.
Results may differ from a plain program's by a relative error of at most 0.028.
The roundings to bfloat16 on the way count: a program that leaves them out, or rounds other values in their place, can miss the bound.
Values may be sent and summed in bfloat16 or wider, within the bound.
No kernel may reach another device: no remote copies, remote signals or barrier semaphores. Data moves between devices by JAX's collectives and lax.ppermute only.
A program may use at most 128 MiB of HBM per device.

v0:
```python
import math
import jax
import jax.numpy as jnp
from jax import lax
from jax.sharding import PartitionSpec as P

EHD = 80
HD = 128
IMAGES = 4
EPSILON = 1e-05


def layer_norm(values, gain_vector):
    mean_value = jnp.mean(values, axis=-1, keepdims=True)
    centered = values - mean_value
    variance = jnp.mean(centered * centered, axis=-1, keepdims=True)
    return centered * lax.rsqrt(variance + EPSILON) * gain_vector


def rms_norm(values, gain_vector):
    square_mean = jnp.mean(values * values, axis=-1, keepdims=True)
    return values * lax.rsqrt(square_mean + EPSILON) * gain_vector


def on_device(
    patches,
    enc_gain,
    enc_qkv,
    enc_out,
    cross_kv,
    key_gain,
    dec_hidden,
    dec_gain,
    query_weight,
    query_gain,
    image_of_row,
    valid_count,
):
    tensor_count = lax.axis_size("tensor")
    seq_count = lax.axis_size("seq")
    patch_rows = patches.shape[0]
    deal_block = patch_rows * seq_count
    gathered = lax.all_gather(patches, "tensor", axis=0, tiled=True)
    row_count = gathered.shape[0]
    normed = layer_norm(gathered.astype(jnp.float32), enc_gain).astype(jnp.bfloat16)
    local_width = enc_qkv.shape[2]
    local_heads = local_width // EHD
    query_part = (
        jnp.dot(normed, enc_qkv[0], preferred_element_type=jnp.float32)
        .astype(jnp.bfloat16)
        .reshape(row_count, local_heads, EHD)
    )
    key_part = jnp.dot(normed, enc_qkv[1], preferred_element_type=jnp.float32).astype(jnp.bfloat16)
    value_part = jnp.dot(normed, enc_qkv[2], preferred_element_type=jnp.float32).astype(
        jnp.bfloat16
    )

    def patch_number(gathered_index):
        shard_number = gathered_index // row_count
        within = gathered_index % row_count
        source_tensor = within // patch_rows
        source_row = within % patch_rows
        source_group = shard_number // seq_count
        source_seq = shard_number % seq_count
        return (
            (source_group * tensor_count + source_tensor) * seq_count + source_seq
        ) * patch_rows + source_row

    def image_number(patch_index):
        return patch_index // deal_block % IMAGES

    own_index = jnp.arange(row_count, dtype=jnp.int32)
    own_shard = lax.axis_index("group") * seq_count + lax.axis_index("seq")
    query_image = image_number(patch_number(own_shard * row_count + own_index))
    running_max = jnp.full((local_heads, row_count), -1e30, jnp.float32)
    key_shard = lax.all_gather(key_part, ("group", "seq"), axis=0, tiled=True)
    value_shard = lax.all_gather(value_part, ("group", "seq"), axis=0, tiled=True)
    piece_rows = key_shard.shape[0]
    key_index = jnp.arange(piece_rows, dtype=jnp.int32)
    key_image = image_number(patch_number(key_index))
    same_image = (query_image[:, None] == key_image[None, :])[None]
    key_heads = key_shard.reshape(piece_rows, local_heads, EHD)
    value_heads = value_shard.reshape(piece_rows, local_heads, EHD)
    scores = jnp.einsum(
        "rhd,khd->hrk", query_part, key_heads, preferred_element_type=jnp.float32
    ) / math.sqrt(EHD)
    masked = jnp.where(same_image, scores, jnp.full_like(scores, -1e30))
    new_max = jnp.maximum(running_max, jnp.max(masked, axis=-1))
    weights = jnp.where(same_image, jnp.exp(scores - new_max[..., None]), jnp.zeros_like(scores))
    new_sum = jnp.sum(weights, axis=-1)
    new_mix = jnp.einsum(
        "hrk,khd->hrd",
        weights.astype(jnp.bfloat16),
        value_heads,
        preferred_element_type=jnp.float32,
    )
    folded = (new_max, new_sum, new_mix)
    final_max, final_sum, final_mix = folded
    attended = (final_mix / final_sum[..., None]).astype(jnp.bfloat16)
    attended = attended.transpose(1, 0, 2).reshape(row_count, local_width)
    total_out = lax.psum(
        jnp.dot(attended, enc_out, preferred_element_type=jnp.float32).astype(jnp.bfloat16),
        "tensor",
    ).astype(jnp.float32)
    encoded = (gathered.astype(jnp.float32) + total_out).astype(jnp.bfloat16)
    kv_local = cross_kv.shape[1] // (2 * HD)
    cross_proj = jnp.dot(encoded, cross_kv, preferred_element_type=jnp.float32).reshape(
        row_count, kv_local, 2, HD
    )
    cross_keys = rms_norm(cross_proj[:, :, 0], key_gain)
    kv_slab = (
        jnp.stack([cross_keys, cross_proj[:, :, 1]], axis=2)
        .astype(jnp.bfloat16)
        .reshape(row_count, kv_local * 2 * HD)
    )
    every_slab = lax.all_gather(kv_slab, ("group", "seq"), axis=0, tiled=True)
    dec_rows = dec_hidden.shape[0]
    dec_normed = rms_norm(dec_hidden.astype(jnp.float32), dec_gain).astype(jnp.bfloat16)
    query_local = query_weight.shape[1] // HD
    group_size = query_local // kv_local
    queries = jnp.dot(dec_normed, query_weight, preferred_element_type=jnp.float32).reshape(
        dec_rows, query_local, HD
    )
    queries = (rms_norm(queries, query_gain) / math.sqrt(HD)).astype(jnp.bfloat16)
    queries = queries.reshape(dec_rows, kv_local, group_size, HD)
    slab_rows = every_slab.shape[0]
    slab_view = every_slab.reshape(slab_rows, kv_local, 2, HD)
    patch_index = patch_number(jnp.arange(slab_rows, dtype=jnp.int32))
    slab_image = image_number(patch_index)
    slab_position = patch_index // (deal_block * IMAGES) * deal_block + patch_index % deal_block
    allowed = (slab_image[None, :] == image_of_row[:, None]) & (
        slab_position[None, :] < valid_count[:, None]
    )
    scores = jnp.einsum(
        "rgqd,kgd->gqrk", queries, slab_view[:, :, 0], preferred_element_type=jnp.float32
    )
    weights = jnp.where(allowed[None, None], jnp.exp(scores), jnp.zeros_like(scores))
    weight_sum = jnp.sum(weights, axis=-1)
    mixture = jnp.einsum(
        "gqrk,kgd->rgqd",
        weights.astype(jnp.bfloat16),
        slab_view[:, :, 1],
        preferred_element_type=jnp.float32,
    )
    result = mixture / weight_sum.transpose(2, 0, 1)[..., None]
    return result.astype(jnp.bfloat16).reshape(dec_rows, query_local * HD)


def solution(mesh):
    in_specs = (
        P(("group", "tensor", "seq"), None),
        P(),
        P(None, None, "tensor"),
        P("tensor", None),
        P(None, "tensor"),
        P(),
        P(("group", "seq"), None),
        P(),
        P(None, "tensor"),
        P(),
        P(("group", "seq")),
        P(("group", "seq")),
    )
    out_specs = P(("group", "seq"), "tensor")
    return jax.shard_map(
        on_device, mesh=mesh, in_specs=in_specs, out_specs=out_specs, check_vma=False
    )
```

profile of v0, /device:TPU:1, one launch (start us, length us, event | category | flops | bytes accessed | tf_op | source)
XLA Modules:
  0.0 340.4 jit_solution(16745044006763906302)
XLA Ops:
  6.5 26.6 %all_gather.12 = bf16[256,1280]{1,0:T(8,128)(2,1)S(1)} all-gather(bf16[32,1280]{1,0:T(8,128)(2,1)} %param.12), channel_id=1, replica_groups=mesh['group'=8,'tensor'=8,'seq'=4] {'tensor'}, dimensions={0}, use_global_device_ids=true | all-gather | bytes 737280 | tf_op jit(solution)/shard_map/all_gather | solution.py:43
  33.1 0.2 convert_reduce_fusion
  33.3 0.3 fusion.22
  33.6 1.0 fusion.24
  34.6 2.0 convolution_convert_fusion.2
  36.6 0.0 all-gather.4.cloned.1.call-update
  36.6 0.0 all-gather.6.cloned.1.call-start
  36.7 0.0 copy-done.9
  36.7 1.0 convolution_convert_fusion.1
  37.7 0.0 all-gather.6.cloned.1.call-update
  37.7 0.0 all-reduce.2.cloned.1.call-start
  37.8 0.1 add_select_fusion.2
  37.9 0.4 convolution_convert_fusion.3
  38.3 1.2 broadcast_compare_fusion
  39.5 62.9 %all-gather.4.cloned.1.call-done = bf16[8192,160]{0,1:T(8,128)(2,1)} async-done(((bf16[256,160]{0,1:T(8,128)(2,1)}), bf16[8192,160]{0,1:T(8,128)(2,1)}) %all-gather.4.cloned.1.call-update) | async-done | bytes 2621456 | tf_op jit(solution)/shard_map/all_gather | solution.py:76
  102.4 5.6 %select_reduce_fusion = (f32[2,256]{1,0:T(2,128)S(1)}, f32[2,256,8192]{2,1,0:T(8,128)S(1)}) fusion(pred[256,8192]{1,0:T(8,128)(4,1)S(1)} %broadcast_compare_fusion, bf16[256,2,80]{0,2,1:T(8,128)(2,1)S(1)} %bitcast.128, bf16[8192,2,80]{0,2,1:T(8,128)(2,1)} %bitcast.126), kind=kOutput, calls=%fused_computation.2 | convolution fusion | flops 683671040 | bytes 21579776 | tf_op jit(solution)/shard_map/rhd,khd->hrk/dot_general | solution.py:84
  108.0 5.7 %copy-done.1 = f32[2,256,8192]{2,1,0:T(8,128)} copy-done((f32[2,256,8192]{2,1,0:T(8,128)}, f32[2,256,8192]{2,1,0:T(8,128)S(1)}, u32[]{:S(2)}) %copy-start.1) | copy-done | bytes 16777240
  113.7 4.8 %fusion.2 = f32[2,256]{1,0:T(2,128)S(1)} fusion(f32[2,256,8192]{2,1,0:T(8,128)S(1)} %get-tuple-element.6, f32[2,256]{1,0:T(2,128)S(1)} %broadcast_maximum_fusion, pred[256,8192]{1,0:T(8,128)(4,1)S(1)} %broadcast_compare_fusion), kind=kLoop, calls=%fused_computation.5 | loop fusion | flops 16776704 | bytes 18878464 | tf_op jit(solution)/shard_map/reduce_sum | solution.py:90
  118.5 41.9 %all-gather.6.cloned.1.call-done = bf16[8192,160]{0,1:T(8,128)(2,1)} async-done(((bf16[256,160]{0,1:T(8,128)(2,1)}), bf16[8192,160]{0,1:T(8,128)(2,1)}) %all-gather.6.cloned.1.call-update) | async-done | bytes 2621456 | tf_op jit(solution)/shard_map/all_gather | solution.py:77
  160.4 8.5 %fusion.35 = bf16[256,2,80]{0,2,1:T(8,128)(2,1)S(1)} fusion(bf16[8192,2,80]{0,2,1:T(8,128)(2,1)} %bitcast.127, f32[2,256,8192]{2,1,0:T(8,128)} %copy-done.1, f32[2,256]{1,0:T(2,128)S(1)} %broadcast_maximum_fusion, pred[256,8192]{1,0:T(8,128)(4,1)S(1)} %broadcast_compare_fusion, f32[256,2]{0,1:T(2,128)S(1)} %bitcast.123), kind=kOutput, calls=%fused_computation.42 | convolution fusion | flops 687947776 | bytes 21581824 | tf_op jit(solution)/shard_map/hrk,khd->hrd/dot_general | solution.py:91
  168.9 0.0 copy-start.6
  168.9 0.0 copy-start.2
  168.9 0.0 copy-start.10
  169.0 1.2 convolution_convert_fusion
  170.2 0.0 all-reduce.2.cloned.1.call-update
  170.2 0.2 all-gather.8.cloned.1.call-start
  170.4 74.0 %all-reduce.2.cloned.1.call-done = bf16[256,1280]{1,0:T(8,128)(2,1)} async-done(((bf16[256,1280]{1,0:T(8,128)(2,1)}), bf16[256,1280]{1,0:T(8,128)(2,1)}) %all-reduce.2.cloned.1.call-update) | async-done | bytes 655376 | tf_op jit(solution)/shard_map/psum | solution.py:101
  244.4 1.5 fusion.44
  246.0 0.1 multiply_convert_fusion
  246.1 0.7 pad_maximum_fusion
  246.8 0.0 all-gather.8.cloned.1.call-update
  246.8 0.5 fusion.12
  247.3 0.0 copy-start.7
  247.3 0.0 copy-start.4
  247.4 0.0 copy-start.5
  247.4 5.4 %fusion.100 = (f32[128,512]{1,0:T(8,128)S(1)}, f32[128,512]{1,0:T(8,128)}) fusion(bf16[8192,512]{1,0:T(8,128)(2,1)} %param.20, bf16[128,8192]{1,0:T(8,128)(2,1)S(1)} %copy-done.2, f32[8192]{0:T(1024)S(1)} %copy-done.10, f32[128]{0:T(128)S(1)} %add_rsqrt_fusion.3), kind=kOutput, calls=%fused_computation.160 | convolution fusion | flops 1078001664 | bytes 11043328 | tf_op jit(solution)/shard_map/dot_general | solution.py:121
  252.8 0.1 mul.214
  252.9 0.2 reduce_sum.70
  253.1 0.1 fusion.73
  253.2 0.0 copy-done.4
  253.2 0.0 copy-done.5
  253.2 2.8 compare_and_fusion
  256.0 58.9 %all-gather.8.cloned.1.call-done = bf16[8192,256]{0,1:T(8,128)(2,1)} async-done(((bf16[256,256]{0,1:T(8,128)(2,1)}), bf16[8192,256]{0,1:T(8,128)(2,1)}) %all-gather.8.cloned.1.call-update) | async-done | bytes 4194320 | tf_op jit(solution)/shard_map/all_gather | solution.py:116
  314.9 0.2 mul.215
  315.1 10.6 %fusion = (f32[4,128]{1,0:T(4,128)S(1)}, f32[8192,128,4]{1,0,2:T(8,128)}) fusion(pred[128,8192]{0,1:T(8,128)(4,1)S(1)} %compare_and_fusion, bf16[8192,1,2,128]{0,3,2,1:T(8,128)(2,1)} %bitcast.124, f32[128,512]{1,0:T(8,128)} %get-tuple-element.8, f32[16,8,4,128]{3,2,1,0:T(4,128)S(1)} %bitcast.120, f32[512]{0:T(512)S(1)} %broadcast_bitcast_fusion), kind=kOutput, calls=%fused_computation.3 | convolution fusion | flops 1082392064 | bytes 20451328 | tf_op jit(solution)/shard_map/rgqd,kgd->gqrk/dot_general | solution.py:134
  325.7 0.0 copy-done.8
  325.7 7.4 %fusion.41 = bf16[128,1,4,128]{0,3,2,1:T(8,128)(2,1)S(1)} fusion(f32[8192,128,4]{1,0,2:T(8,128)} %get-tuple-element.10, pred[128,8192]{0,1:T(8,128)(4,1)S(1)} %compare_and_fusion, bf16[8192,1,2,128]{0,3,2,1:T(8,128)(2,1)S(1)} %bitcast.125, f32[128,4]{0,1:T(4,128)S(1)} %bitcast.129), kind=kOutput, calls=%fused_computation.44 | convolution fusion | flops 1082261504 | bytes 20056064 | tf_op jit(solution)/shard_map/gqrk,kgd->rgqd/dot_general | solution.py:139
  333.1 0.8 copy.31
  (22 shorter events, 0.2 us)
Async XLA Ops:
  6.5 237.9 %copy-start = (bf16[1280,256]{1,0:T(8,128)(2,1)S(1)}, bf16[1280,256]{1,0:T(8,128)(2,1)}, u32[]{:S(2)}) copy-start(bf16[1280,256]{1,0:T(8,128)(2,1)} %param.16) | copy-start | bytes 1966084
  6.5 30.2 %copy-start.9 = (bf16[3,1280,160]{1,2,0:T(8,128)(2,1)S(1)}, bf16[3,1280,160]{1,2,0:T(8,128)(2,1)}, u32[]{:S(2)}) copy-start(bf16[3,1280,160]{1,2,0:T(8,128)(2,1)} %param.14) | copy-start | bytes 3686404
  6.5 95.9 %all-gather.4.cloned.1.call-start = ((), (), s32[]{:S(2)}) async-start(), calls=%async_computation | async-start | bytes 2703360 | tf_op jit(solution)/shard_map/all_gather | solution.py:76
  36.6 123.8 %all-gather.6.cloned.1.call-start = ((), (), s32[]{:S(2)}) async-start(), calls=%async_computation.1 | async-start | bytes 2703360 | tf_op jit(solution)/shard_map/all_gather | solution.py:77
  37.7 206.7 %all-reduce.2.cloned.1.call-start = ((), (), s32[]{:S(2)}) async-start(), calls=%async_computation.2 | async-start | bytes 1310720 | tf_op jit(solution)/shard_map/psum | solution.py:101
  108.0 5.7 %copy-start.1 = (f32[2,256,8192]{2,1,0:T(8,128)}, f32[2,256,8192]{2,1,0:T(8,128)S(1)}, u32[]{:S(2)}) copy-start(f32[2,256,8192]{2,1,0:T(8,128)S(1)} %get-tuple-element.6) | copy-start | bytes 50331652
  160.4 8.6 %copy-start.3 = (bf16[160,1280]{1,0:T(8,128)(2,1)S(1)}, bf16[160,1280]{1,0:T(8,128)(2,1)}, u32[]{:S(2)}) copy-start(bf16[160,1280]{1,0:T(8,128)(2,1)} %param.15) | copy-start | bytes 1228804
  168.9 77.1 %copy-start.6 = (f32[128]{0:T(128)S(1)}, f32[128]{0:T(128)}, u32[]{:S(2)}) copy-start(f32[128]{0:T(128)} %param.17) | copy-start | bytes 1540
  168.9 77.9 %copy-start.2 = (bf16[128,8192]{1,0:T(8,128)(2,1)S(1)}, bf16[128,8192]{1,0:T(8,128)(2,1)}, u32[]{:S(2)}) copy-start(bf16[128,8192]{1,0:T(8,128)(2,1)} %param.18) | copy-start | bytes 6291460
  168.9 78.4 %copy-start.10 = (f32[8192]{0:T(1024)S(1)}, f32[8192]{0:T(1024)}, u32[]{:S(2)}) copy-start(f32[8192]{0:T(1024)} %param.19) | copy-start | bytes 98308
  170.2 144.7 %all-gather.8.cloned.1.call-start = ((), (), s32[]{:S(2)}) async-start(), calls=%async_computation.3 | async-start | bytes 4325376 | tf_op jit(solution)/shard_map/all_gather | solution.py:116
  247.3 5.8 %copy-start.7 = (f32[128]{0:T(128)S(1)}, f32[128]{0:T(128)}, u32[]{:S(2)}) copy-start(f32[128]{0:T(128)} %param.21) | copy-start | bytes 1540
  247.3 5.8 %copy-start.4 = (s32[128]{0:T(128)S(1)}, s32[128]{0:T(128)}, u32[]{:S(2)}) copy-start(s32[128]{0:T(128)} %param.23) | copy-start | bytes 1540
  247.4 5.8 %copy-start.5 = (s32[128]{0:T(128)S(1)}, s32[128]{0:T(128)}, u32[]{:S(2)}) copy-start(s32[128]{0:T(128)} %param.22) | copy-start | bytes 1540
  315.1 10.6 %copy-start.8 = (bf16[8192,256]{0,1:T(8,128)(2,1)S(1)}, bf16[8192,256]{0,1:T(8,128)(2,1)}, u32[]{:S(2)}) copy-start(bf16[8192,256]{0,1:T(8,128)(2,1)} %all-gather.8.cloned.1.call-done) | copy-start | bytes 12582916
Sparse Core Ops, SparseCore 0:
  36.8 65.6 all-gather.3
  104.9 55.4 all-gather.5
  170.3 74.0 all-reduce.1
  246.9 67.8 all-gather.7
where the time goes:
time: 341 us; the launch traced here: 340 us
  waiting for transfers between devices  238 us (70%)
  matrix products  43.6 us (13%)
  blocking collectives  26.6 us (8%)
  between operations  13.4 us (4%)
  other arithmetic  11.9 us (3%)
  local copies, waits for them, and re-layouts  6.82 us (2%)
    psum x1, waiting for transfers between devices, on_device(): lax.psum(jnp.dot(attended, enc_out, preferred_element_type=jnp.float32).a...  74 us
    all_gather x1, waiting for transfers between devices, on_device(): key_shard = lax.all_gather(key_part, ('group', 'seq'), axis=0, tiled=True)  62.9 us
    all_gather x1, waiting for transfers between devices, on_device(): every_slab = lax.all_gather(kv_slab, ('group', 'seq'), axis=0, tiled=True)  58.9 us
    all_gather x1, waiting for transfers between devices, on_device(): lax.all_gather(value_part, ('group', 'seq'), axis=0, tiled=True)  41.9 us
    all_gather x1, blocking collectives, on_device(): gathered = lax.all_gather(patches, 'tensor', axis=0, tiled=True)  26.6 us
    dot_general x1, matrix products, on_device(): jnp.einsum('rgqd,kgd->gqrk', queries, slab_view[:, :, 0], preferred_eleme...  10.6 us
    dot_general x1, matrix products, on_device(): jnp.einsum('hrk,khd->hrd', weights.astype(jnp.bfloat16), value_heads, pre...  8.5 us
    dot_general x1, matrix products, on_device(): jnp.einsum('gqrk,kgd->rgqd', weights.astype(jnp.bfloat16), slab_view[:, :...  7.39 us
  transfers between devices with their start and end apart: 4, of which 4 were waited for; matrix products, arithmetic and copies ran while one was open for 7% of the time, Pallas kernels for 0%

commit v1 on v0

--- a/solution.py
+++ b/solution.py
@@ -8,6 +8,13 @@
 HD = 128
 IMAGES = 4
 EPSILON = 1e-05
+
+
+def swapped_in(x, mesh_axis, d):
+    peers = lax.axis_size(mesh_axis)
+    blocks = jnp.stack([x for _ in range(peers)])
+    blocks = lax.all_to_all(blocks, mesh_axis, split_axis=0, concat_axis=0)
+    return jnp.concatenate(blocks, axis=d)
 
 
 def layer_norm(values, gain_vector):
@@ -113,7 +120,7 @@
         .astype(jnp.bfloat16)
         .reshape(row_count, kv_local * 2 * HD)
     )
-    every_slab = lax.all_gather(kv_slab, ("group", "seq"), axis=0, tiled=True)
+    every_slab = swapped_in(kv_slab, ("group", "seq"), 0)
     dec_rows = dec_hidden.shape[0]
     dec_normed = rms_norm(dec_hidden.astype(jnp.float32), dec_gain).astype(jnp.bfloat16)
     query_local = query_weight.shape[1] // HD

time: 341 us -> 399 us (1.17)
  waiting for transfers between devices: 238 us -> 268 us
  local copies, waits for them, and re-layouts: 6.82 us -> 23.2 us
  starting transfers between devices: 0.31 us -> 14.5 us
    all_to_all x0 -> x1, waiting for transfers between devices: none -> 88.4 us  [swapped_in(): blocks = lax.all_to_all(blocks, mesh_axis, split_axis=0, concat_axis=0)]
    all_gather x1 -> x0, waiting for transfers between devices: 58.9 us -> none  [on_device(): every_slab = lax.all_gather(kv_slab, ('group', 'seq'), axis=0, tiled=True)]
    all_to_all x0 -> x1, starting transfers between devices: none -> 14.4 us  [swapped_in(): blocks = lax.all_to_all(blocks, mesh_axis, split_axis=0, concat_axis=0)]
    another operation x0 -> x2, local copies, waits for them, and re-layouts: none -> 9.86 us  [the longest x1 7.41 us: on_device(): slab_view = every_slab.reshape(slab_rows, kv_local, 2, HD)]
    all_to_all x0 -> x1, local copies, waits for them, and re-layouts: none -> 6.53 us  [swapped_in(): blocks = lax.all_to_all(blocks, mesh_axis, split_axis=0, concat_axis=0)]
  transfers between devices with their start and end apart: 4 -> 4, of which waited for: 4 -> 4; matrix products, arithmetic and copies ran while one was open for 7% -> 5% of each run, Pallas kernels for 0% -> 0%
where the time goes in v1:
time: 399 us; the launch traced here: 398 us
  waiting for transfers between devices  268 us (67%)
  matrix products  42 us (11%)
  blocking collectives  26.6 us (7%)
  local copies, waits for them, and re-layouts  23.2 us (6%)
  starting transfers between devices  14.5 us (4%)
  between operations  13.4 us (3%)
  other arithmetic  11.3 us (3%)
    all_to_all x1, waiting for transfers between devices, swapped_in(): blocks = lax.all_to_all(blocks, mesh_axis, split_axis=0, concat_axis=0)  88.4 us
    psum x1, waiting for transfers between devices, on_device(): lax.psum(jnp.dot(attended, enc_out, preferred_element_type=jnp.float32).a...  74.2 us
    all_gather x1, waiting for transfers between devices, on_device(): key_shard = lax.all_gather(key_part, ('group', 'seq'), axis=0, tiled=True)  62.9 us
    all_gather x1, waiting for transfers between devices, on_device(): lax.all_gather(value_part, ('group', 'seq'), axis=0, tiled=True)  41.9 us
    all_gather x1, blocking collectives, on_device(): gathered = lax.all_gather(patches, 'tensor', axis=0, tiled=True)  26.6 us
    all_to_all x1, starting transfers between devices, swapped_in(): blocks = lax.all_to_all(blocks, mesh_axis, split_axis=0, concat_axis=0)  14.4 us
    dot_general x1, matrix products, on_device(): jnp.einsum('rgqd,kgd->gqrk', queries, slab_view[:, :, 0], preferred_eleme...  9.56 us
    dot_general x1, matrix products, on_device(): jnp.einsum('hrk,khd->hrd', weights.astype(jnp.bfloat16), value_heads, pre...  8.5 us
  transfers between devices with their start and end apart: 4, of which 4 were waited for; matrix products, arithmetic and copies ran while one was open for 5% of the time, Pallas kernels for 0%

profile of v1, /device:TPU:1, one launch (start us, length us, event | category | flops | bytes accessed | tf_op | source)
XLA Modules:
  0.0 398.5 jit_solution(12006192971372563257)
XLA Ops:
  6.5 0.0 copy-start
  6.5 0.0 all-gather.3.cloned.1.call-start
  6.5 26.6 %all_gather.9 = bf16[256,1280]{1,0:T(8,128)(2,1)S(1)} all-gather(bf16[32,1280]{1,0:T(8,128)(2,1)} %param.12), channel_id=1, replica_groups=mesh['group'=8,'tensor'=8,'seq'=4] {'tensor'}, dimensions={0}, use_global_device_ids=true | all-gather | bytes 737280 | tf_op jit(solution)/shard_map/all_gather | solution.py:50
  33.1 0.2 convert_reduce_fusion
  33.3 0.3 fusion.22
  33.6 1.0 fusion.24
  34.6 2.0 convolution_convert_fusion.2
  36.6 0.0 all-gather.3.cloned.1.call-update
  36.6 0.0 all-gather.5.cloned.1.call-start
  36.7 0.0 copy-done.10
  36.7 1.0 convolution_convert_fusion.1
  37.7 0.0 all-gather.5.cloned.1.call-update
  37.7 0.0 all-reduce.2.cloned.1.call-start
  37.8 0.1 add_select_fusion.2
  37.9 0.4 convolution_convert_fusion.3
  38.3 1.2 broadcast_compare_fusion
  39.5 62.9 %all-gather.3.cloned.1.call-done = bf16[8192,160]{0,1:T(8,128)(2,1)} async-done(((bf16[256,160]{0,1:T(8,128)(2,1)}), bf16[8192,160]{0,1:T(8,128)(2,1)}) %all-gather.3.cloned.1.call-update) | async-done | bytes 2621456 | tf_op jit(solution)/shard_map/all_gather | solution.py:83
  102.4 5.6 %select_reduce_fusion = (f32[2,256]{1,0:T(2,128)S(1)}, f32[2,256,8192]{2,1,0:T(8,128)S(1)}) fusion(pred[256,8192]{1,0:T(8,128)(4,1)S(1)} %broadcast_compare_fusion, bf16[256,2,80]{0,2,1:T(8,128)(2,1)S(1)} %bitcast.127, bf16[8192,2,80]{0,2,1:T(8,128)(2,1)} %bitcast.125), kind=kOutput, calls=%fused_computation.2 | convolution fusion | flops 683671040 | bytes 21579776 | tf_op jit(solution)/shard_map/rhd,khd->hrk/dot_general | solution.py:91
  108.0 5.7 %copy-done.2 = f32[2,256,8192]{2,1,0:T(8,128)} copy-done((f32[2,256,8192]{2,1,0:T(8,128)}, f32[2,256,8192]{2,1,0:T(8,128)S(1)}, u32[]{:S(2)}) %copy-start.2) | copy-done | bytes 16777240
  113.7 4.8 %fusion.2 = f32[2,256]{1,0:T(2,128)S(1)} fusion(f32[2,256,8192]{2,1,0:T(8,128)S(1)} %get-tuple-element.6, f32[2,256]{1,0:T(2,128)S(1)} %broadcast_maximum_fusion, pred[256,8192]{1,0:T(8,128)(4,1)S(1)} %broadcast_compare_fusion), kind=kLoop, calls=%fused_computation.5 | loop fusion | flops 16776704 | bytes 18878464 | tf_op jit(solution)/shard_map/reduce_sum | solution.py:97
  118.5 41.9 %all-gather.5.cloned.1.call-done = bf16[8192,160]{0,1:T(8,128)(2,1)} async-done(((bf16[256,160]{0,1:T(8,128)(2,1)}), bf16[8192,160]{0,1:T(8,128)(2,1)}) %all-gather.5.cloned.1.call-update) | async-done | bytes 2621456 | tf_op jit(solution)/shard_map/all_gather | solution.py:84
  160.4 8.5 %fusion.35 = bf16[256,2,80]{0,2,1:T(8,128)(2,1)S(1)} fusion(bf16[8192,2,80]{0,2,1:T(8,128)(2,1)} %bitcast.126, f32[2,256,8192]{2,1,0:T(8,128)} %copy-done.2, f32[2,256]{1,0:T(2,128)S(1)} %broadcast_maximum_fusion, pred[256,8192]{1,0:T(8,128)(4,1)S(1)} %broadcast_compare_fusion, f32[256,2]{0,1:T(2,128)S(1)} %bitcast.124), kind=kOutput, calls=%fused_computation.42 | convolution fusion | flops 687947776 | bytes 21581824 | tf_op jit(solution)/shard_map/hrk,khd->hrd/dot_general | solution.py:98
  168.9 0.0 copy-start.8
  168.9 1.2 convolution_convert_fusion
  170.2 0.0 all-reduce.2.cloned.1.call-update
  170.2 74.2 %all-reduce.2.cloned.1.call-done = bf16[256,1280]{1,0:T(8,128)(2,1)} async-done(((bf16[256,1280]{1,0:T(8,128)(2,1)}), bf16[256,1280]{1,0:T(8,128)(2,1)}) %all-reduce.2.cloned.1.call-update) | async-done | bytes 655376 | tf_op jit(solution)/shard_map/psum | solution.py:108
  244.4 1.5 fusion.44
  246.0 0.1 multiply_convert_fusion
  246.1 2.4 stack.8
  248.6 14.4 %all-to-all-start = ((bf16[32,256,256]{1,2,0:T(8,128)(2,1)}), bf16[32,256,256]{1,2,0:T(8,128)(2,1)}, u32[]{:S(2)}, u32[]{:S(2)}) async-start(bf16[32,256,256]{1,2,0:T(8,128)(2,1)} %stack.8), calls=%async_computation | async-start | bytes 8388608 | tf_op jit(solution)/shard_map/all_to_all | solution.py:16
  263.0 0.0 copy-done.4
  263.1 0.5 fusion.12
  263.6 0.0 copy-start.9
  263.6 0.0 copy-start.6
  263.6 0.0 copy-start.7
  263.6 4.7 %fusion.100 = (f32[128,512]{1,0:T(8,128)S(1)}, f32[128,512]{1,0:T(8,128)S(1)}) fusion(bf16[8192,512]{1,0:T(8,128)(2,1)} %param.20, bf16[128,8192]{1,0:T(8,128)(2,1)S(1)} %copy-done.4, f32[8192]{0:T(1024)S(1)} %copy-done.11, f32[128]{0:T(128)S(1)} %add_rsqrt_fusion.3), kind=kOutput, calls=%fused_computation.160 | convolution fusion | flops 1078001664 | bytes 11043328 | tf_op jit(solution)/shard_map/dot_general | solution.py:128
  268.3 0.1 mul.214
  268.4 0.2 reduce_sum.70
  268.6 0.1 fusion.73
  268.8 2.8 compare_and_fusion
  271.5 88.4 %all-to-all-done = bf16[32,256,256]{1,2,0:T(8,128)(2,1)} async-done(((bf16[32,256,256]{1,2,0:T(8,128)(2,1)}), bf16[32,256,256]{1,2,0:T(8,128)(2,1)}, u32[]{:S(2)}, u32[]{:S(2)}) %all-to-all-start) | async-done | bytes 4194336 | tf_op jit(solution)/shard_map/all_to_all | solution.py:16
  360.0 6.5 %copy.33 = bf16[32,256,256]{1,0,2:T(8,128)(2,1)} copy(bf16[32,256,256]{1,2,0:T(8,128)(2,1)} %all-to-all-done) | data formatting | bytes 8388608 | tf_op jit(solution)/shard_map/all_to_all | solution.py:16
  366.5 7.4 %reshape_reshape.3 = bf16[8192,1,2,128]{0,3,2,1:T(8,128)(2,1)} reshape(bf16[32,256,256]{1,0,2:T(8,128)(2,1)} %copy.33) | data formatting | bytes 8388608 | tf_op jit(solution)/shard_map/reshape;reshape | solution.py:134
  373.9 0.2 mul.215
  374.1 9.6 %fusion = (f32[4,128]{1,0:T(4,128)S(1)}, f32[8192,128,4]{1,0,2:T(8,128)}) fusion(pred[128,8192]{0,1:T(8,128)(4,1)S(1)} %compare_and_fusion, bf16[8192,1,2,128]{0,3,2,1:T(8,128)(2,1)} %reshape_reshape.3, f32[128,512]{1,0:T(8,128)S(1)} %get-tuple-element.8, f32[16,8,4,128]{3,2,1,0:T(4,128)S(1)} %bitcast.121, f32[512]{0:T(512)S(1)} %broadcast_bitcast_fusion), kind=kOutput, calls=%fused_computation.3 | convolution fusion | flops 1082392064 | bytes 20451328 | tf_op jit(solution)/shard_map/rgqd,kgd->gqrk/dot_general | solution.py:141
  383.7 7.5 %fusion.41 = bf16[128,1,4,128]{0,3,2,1:T(8,128)(2,1)S(1)} fusion(f32[8192,128,4]{1,0,2:T(8,128)} %get-tuple-element.10, pred[128,8192]{0,1:T(8,128)(4,1)S(1)} %compare_and_fusion, bf16[8192,1,2,128]{0,3,2,1:T(8,128)(2,1)S(1)} %copy-done.3, f32[128,4]{0,1:T(4,128)S(1)} %bitcast.128), kind=kOutput, calls=%fused_computation.44 | convolution fusion | flops 1082261504 | bytes 20056064 | tf_op jit(solution)/shard_map/gqrk,kgd->rgqd/dot_general | solution.py:146
  391.1 0.8 copy.39
  391.9 0.0 copy-done.1
  (26 shorter events, 0.2 us)
Async XLA Ops:
  6.5 237.9 %copy-start = (bf16[1280,256]{1,0:T(8,128)(2,1)S(1)}, bf16[1280,256]{1,0:T(8,128)(2,1)}, u32[]{:S(2)}) copy-start(bf16[1280,256]{1,0:T(8,128)(2,1)} %param.16) | copy-start | bytes 1966084
  6.5 30.2 %copy-start.10 = (bf16[3,1280,160]{1,2,0:T(8,128)(2,1)S(1)}, bf16[3,1280,160]{1,2,0:T(8,128)(2,1)}, u32[]{:S(2)}) copy-start(bf16[3,1280,160]{1,2,0:T(8,128)(2,1)} %param.14) | copy-start | bytes 3686404
  6.5 95.9 %all-gather.3.cloned.1.call-start = ((), (), s32[]{:S(2)}) async-start(), calls=%async_computation.1 | async-start | bytes 2703360 | tf_op jit(solution)/shard_map/all_gather | solution.py:83
  36.6 123.8 %all-gather.5.cloned.1.call-start = ((), (), s32[]{:S(2)}) async-start(), calls=%async_computation.2 | async-start | bytes 2703360 | tf_op jit(solution)/shard_map/all_gather | solution.py:84
  37.7 206.7 %all-reduce.2.cloned.1.call-start = ((), (), s32[]{:S(2)}) async-start(), calls=%async_computation.3 | async-start | bytes 1310720 | tf_op jit(solution)/shard_map/psum | solution.py:108
  108.0 5.7 %copy-start.2 = (f32[2,256,8192]{2,1,0:T(8,128)}, f32[2,256,8192]{2,1,0:T(8,128)S(1)}, u32[]{:S(2)}) copy-start(f32[2,256,8192]{2,1,0:T(8,128)S(1)} %get-tuple-element.6) | copy-start | bytes 50331652
  160.4 8.5 %copy-start.5 = (bf16[160,1280]{1,0:T(8,128)(2,1)S(1)}, bf16[160,1280]{1,0:T(8,128)(2,1)}, u32[]{:S(2)}) copy-start(bf16[160,1280]{1,0:T(8,128)(2,1)} %param.15) | copy-start | bytes 1228804
  168.9 77.1 %copy-start.8 = (f32[128]{0:T(128)S(1)}, f32[128]{0:T(128)}, u32[]{:S(2)}) copy-start(f32[128]{0:T(128)} %param.17) | copy-start | bytes 1540
  248.6 14.4 %copy-start.4 = (bf16[128,8192]{1,0:T(8,128)(2,1)S(1)}, bf16[128,8192]{1,0:T(8,128)(2,1)}, u32[]{:S(2)}) copy-start(bf16[128,8192]{1,0:T(8,128)(2,1)} %param.18) | copy-start | bytes 6291460
  248.6 15.0 %copy-start.11 = (f32[8192]{0:T(1024)S(1)}, f32[8192]{0:T(1024)}, u32[]{:S(2)}) copy-start(f32[8192]{0:T(1024)} %param.19) | copy-start | bytes 98308
  248.6 111.4 %all-to-all-start = ((bf16[32,256,256]{1,2,0:T(8,128)(2,1)}), bf16[32,256,256]{1,2,0:T(8,128)(2,1)}, u32[]{:S(2)}, u32[]{:S(2)}) async-start(bf16[32,256,256]{1,2,0:T(8,128)(2,1)} %stack.8), calls=%async_computation | async-start | bytes 8388608 | tf_op jit(solution)/shard_map/all_to_all | solution.py:16
  263.6 5.1 %copy-start.9 = (f32[128]{0:T(128)S(1)}, f32[128]{0:T(128)}, u32[]{:S(2)}) copy-start(f32[128]{0:T(128)} %param.21) | copy-start | bytes 1540
  263.6 5.2 %copy-start.6 = (s32[128]{0:T(128)S(1)}, s32[128]{0:T(128)}, u32[]{:S(2)}) copy-start(s32[128]{0:T(128)} %param.23) | copy-start | bytes 1540
  263.6 5.2 %copy-start.7 = (s32[128]{0:T(128)S(1)}, s32[128]{0:T(128)}, u32[]{:S(2)}) copy-start(s32[128]{0:T(128)} %param.22) | copy-start | bytes 1540
  374.1 9.6 %copy-start.3 = (bf16[8192,1,2,128]{0,3,2,1:T(8,128)(2,1)S(1)}, bf16[8192,1,2,128]{0,3,2,1:T(8,128)(2,1)}, u32[]{:S(2)}) copy-start(bf16[8192,1,2,128]{0,3,2,1:T(8,128)(2,1)} %reshape_reshape.3) | copy-start | bytes 12582916
  383.7 8.2 %copy-start.1 = (bf16[1280,256]{1,0:T(8,128)(2,1)S(1)}, bf16[1280,256]{1,0:T(8,128)(2,1)}, u32[]{:S(2)}) copy-start(bf16[1280,256]{1,0:T(8,128)(2,1)} %param.16) | copy-start | bytes 1966084
Sparse Core Ops, SparseCore 0:
  36.8 65.6 all-gather.2
  104.9 55.4 all-gather.4
  170.3 74.0 all-reduce.1
